TPU v7x, 32 devices: a whole 2x2x4 slice. The times are simulated.
32 devices in a mesh: groups: 2 (over y), blk: 4 (over z), head: 4 (over x, core).
Axes of the slice: x: 2, y: 2, z: 4, core: 2. Of those that a mesh axis runs over, the one named last changes fastest.
Arguments:
- ctx_query: bfloat16 [4096, 8192], P(('groups', 'blk'), 'head'), parts along dimension 0, may hold values from -5 to 5
- ctx_key: bfloat16 [4096, 1024], P(('groups', 'blk'), 'head'), parts along dimension 0, may hold values from -5 to 5
- ctx_value: bfloat16 [4096, 1024], P(('groups', 'blk'), 'head'), parts along dimension 0, may hold values from -4.5 to 4.5
- opt_query: bfloat16 [128, 8192], P(('groups', 'blk'), 'head'), parts along dimension 0, may hold values from -5 to 5
- opt_owner: int32 [128], P('groups'), parts along dimension 0, may hold values from 0 to 3, as said below
- opt_slot: int32 [128], P('groups'), parts along dimension 0, may hold values from 0 to 31, as said below
- opt_length: int32 [128], P('groups'), parts along dimension 0, may hold values from 512 to 2048
Outputs:
- ctx_out: bfloat16 [4096, 8192], P(('groups', 'blk'), 'head'), parts along dimension 0
- opt_out: bfloat16 [256, 8192], P(('groups', 'blk'), 'head'), parts along dimension 0
There are 2 independent parts, one for each index of `groups`. A program takes and returns all parts, laid end to end along the dimension named above; each array names one. Nothing has to cross between parts.
Inputs may be any that keep to these rules, and one draw needn't show every extreme that they name: `opt_owner`: each option token has its own pair of owner block and slot; no block owns more than 32 option tokens, and one block owns exactly 32. `opt_slot`: slots of one owner are distinct.
All inputs are finite; a program needn't handle non-finite values.
Results may differ from a plain program's by a relative error of at most 0.017.
Values may be sent and summed in bfloat16 or wider, within the bound.
A program may use at most 64 MiB of HBM per device.

v0:
```python
import jax
import jax.numpy as jnp
from jax import lax
from jax.sharding import PartitionSpec as P

HD = 128
HQ = 64
KVH = 8
CAP = 32


def from_root(value, axis, root):
    mine = lax.axis_index(axis) == root
    return lax.psum(jnp.where(mine, value, jnp.zeros_like(value)), axis)


def soft_parts(query_head, keys, values, masks, scale):
    scores = []
    for key_part, mask_part in zip(keys, masks):
        raw = (
            jnp.einsum("td,sd->ts", query_head, key_part, preferred_element_type=jnp.float32)
            * scale
        )
        scores.append(jnp.where(mask_part, raw, -1e30))
    top = jnp.max(scores[0], axis=1)
    for extra in scores[1:]:
        top = jnp.maximum(top, jnp.max(extra, axis=1))
    total = jnp.zeros_like(top)
    accum = jnp.zeros((query_head.shape[0], values[0].shape[1]), jnp.float32)
    for score_part, value_part in zip(scores, values):
        expo = jnp.exp(score_part - top[:, None])
        total = total + jnp.sum(expo, axis=1)
        accum = accum + jnp.dot(
            expo.astype(jnp.bfloat16), value_part, preferred_element_type=jnp.float32
        )
    return (accum / total[:, None], top, total)


def body(ctx_query, ctx_key, ctx_value, opt_query, opt_owner, opt_slot, opt_length):
    group_size = HQ // KVH
    scale = HD ** (-0.5)
    block_index = lax.axis_index("blk")
    block_count = lax.axis_size("blk")
    rows = ctx_query.shape[0]
    local_heads = ctx_query.shape[1] // HD
    anchor_key, anchor_value = (from_root(ctx_key, "blk", 0), from_root(ctx_value, "blk", 0))
    spots = jnp.arange(rows, dtype=jnp.int32)
    causal = spots[:, None] >= spots[None, :]
    anchor_mask = jnp.broadcast_to(block_index > 0, (rows, rows))

    def phase_one(head_id, result):
        group = head_id // group_size
        query_head = lax.dynamic_slice_in_dim(ctx_query, head_id * HD, HD, 1)
        key_local = lax.dynamic_slice_in_dim(ctx_key, group * HD, HD, 1)
        value_local = lax.dynamic_slice_in_dim(ctx_value, group * HD, HD, 1)
        key_anchor = lax.dynamic_slice_in_dim(anchor_key, group * HD, HD, 1)
        value_anchor = lax.dynamic_slice_in_dim(anchor_value, group * HD, HD, 1)
        output, top, total = soft_parts(
            query_head,
            (key_anchor, key_local),
            (value_anchor, value_local),
            (anchor_mask, causal),
            scale,
        )
        return lax.dynamic_update_slice_in_dim(result, output.astype(jnp.bfloat16), head_id * HD, 1)

    ctx_out = lax.fori_loop(0, local_heads, phase_one, jnp.zeros(ctx_query.shape, jnp.bfloat16))
    all_queries = lax.all_gather(opt_query, "blk", axis=0, tiled=True)
    options = all_queries.shape[0]
    count = jnp.clip(opt_length - block_index * rows, 0, rows)
    live = count > 0
    visible = spots[None, :] < count[:, None]

    def phase_two(head_id, carry):
        partial_value, stats = carry
        group = head_id // group_size
        query_head = lax.dynamic_slice_in_dim(all_queries, head_id * HD, HD, 1)
        key_local = lax.dynamic_slice_in_dim(ctx_key, group * HD, HD, 1)
        value_local = lax.dynamic_slice_in_dim(ctx_value, group * HD, HD, 1)
        output, top, total = soft_parts(query_head, (key_local,), (value_local,), (visible,), scale)
        output = jnp.where(live[:, None], output, 0.0).astype(jnp.bfloat16)
        stat = jnp.where(live, top + jnp.log(total), -1e30)
        partial_value = lax.dynamic_update_slice_in_dim(partial_value, output, head_id * HD, 1)
        stats = lax.dynamic_update_slice_in_dim(stats, stat[:, None], head_id, 1)
        return (partial_value, stats)

    start = (
        jnp.zeros((options, local_heads * HD), jnp.bfloat16),
        jnp.zeros((options, local_heads), jnp.float32),
    )
    partial_value, stats = lax.fori_loop(0, local_heads, phase_two, start)
    slot_total = CAP * block_count
    where_to = opt_owner * CAP + opt_slot
    top_all = lax.pmax(stats, "blk")
    weight = jnp.exp(stats - top_all)
    weight_sum = lax.psum(weight, "blk")
    share = weight / weight_sum
    term = (
        partial_value.reshape(options, local_heads, HD).astype(jnp.float32) * share[:, :, None]
    ).reshape(options, local_heads * HD)
    buffer = jnp.zeros((slot_total, local_heads * HD), jnp.float32).at[where_to].set(term)
    opt_out = lax.psum_scatter(buffer.astype(jnp.bfloat16), "blk", scatter_dimension=0, tiled=True)
    return (ctx_out, opt_out)


def solution(mesh):
    return jax.shard_map(
        body,
        mesh=mesh,
        in_specs=(
            P(("groups", "blk"), "head"),
            P(("groups", "blk"), "head"),
            P(("groups", "blk"), "head"),
            P(("groups", "blk"), "head"),
            P("groups"),
            P("groups"),
            P("groups"),
        ),
        out_specs=(P(("groups", "blk"), "head"), P(("groups", "blk"), "head")),
        check_vma=False,
    )
```

profile of v0, /device:TPU:0, one launch (start us, length us, event | category | flops | bytes accessed | tf_op | source)
XLA Modules:
  0.0 127.9 jit_solution(5371850114910661687)
XLA Ops:
  7.2 1.9 %broadcast_select_fusion = (bf16[512,256]{1,0:T(8,128)(2,1)}, bf16[512,256]{1,0:T(8,128)(2,1)}) fusion(bf16[512,256]{1,0:T(8,128)(2,1)} %param.13, pred[]{:T(512)S(6)} %eq.4, bf16[512,256]{1,0:T(8,128)(2,1)} %param.12), kind=kLoop, calls=%fused_computation.54 | loop fusion | flops 262144 | bytes 1048577 | tf_op jit(solution)/shard_map/jit(_where)/select_n | solution.py:14
  9.2 15.8 %all_gather.3 = bf16[64,2048]{1,0:T(8,128)(2,1)S(1)} all-gather(bf16[16,2048]{1,0:T(8,128)(2,1)} %param.14), channel_id=1, replica_groups=mesh['groups'=2,'blk'=4,'head'=4] {'blk'}, dimensions={0}, use_global_device_ids=true | all-gather | bytes 327680 | tf_op jit(solution)/shard_map/all_gather | solution.py:68
  25.7 12.9 %while.35 = (s32[]{:T(128)}, bf16[64,2048]{1,0:T(8,128)(2,1)S(1)}, f32[64,16]{0,1:T(8,128)S(1)}, pred[64]{0:T(512)(128)(4,1)S(1)}, bf16[64,2048]{1,0:T(8,128)(2,...) while((s32[]{:T(128)}, bf16[64,2048]{1,0:T(8,128)(2,1)S(1)}, ...), condition=%wide.region_11.12_spmd.clone, body=%wide.region_8.11_spmd.clone.sunk | while | flops 17063952 | bytes 692635 | solution.py:91
  38.6 11.7 %pmax.7 = f32[64,16]{0,1:T(8,128)S(1)} all-reduce(f32[64,16]{0,1:T(8,128)S(1)} %get-tuple-element.425), channel_id=1, replica_groups=mesh['groups'=2,'blk'=4,'head'=4] {'blk'}, use_global_device_ids=true, to_apply=%region_12.13 | all-reduce | flops 1024 | bytes 8192 | tf_op jit(solution)/shard_map/pmax | solution.py:94
  50.4 8.5 %psum.23 = f32[64,16]{0,1:T(8,128)S(1)} all-reduce(f32[64,16]{0,1:T(8,128)S(1)} %subtract_exponential_fusion.3), channel_id=1, replica_groups=mesh['groups'=2,'blk'=4,'head'=4] {'blk'}, use_global_device_ids=true, to_apply=%region_13.14 | all-reduce | flops 1024 | bytes 8192 | tf_op jit(solution)/shard_map/psum | solution.py:96
  59.2 1.3 %scatter_custom_fusion = f32[128,2048]{1,0:T(8,128)S(1)} fusion(s32[64]{0:T(128)S(1)} %compare_select_fusion, f32[8,8,16,128]{3,2,1,0:T(8,128)S(1)} %bitcast.8, bf16[64,2048]{1,0:T(8,128)(2,1)S(1)} %get-tuple-element.424, f32[]{:T(128)} %constant.275.clone.1), kind=kCustom, calls=%fused_computation.50 | custom fusion | flops 262144 | bytes 1835012 | tf_op jit(solution)/shard_map/scatter | solution.py:101
  62.5 57.1 %while.34 = (s32[]{:T(128)}, bf16[512,2048]{1,0:T(8,128)(2,1)S(1)}, bf16[512,2048]{1,0:T(8,128)(2,1)}, bf16[512,256]{1,0:T(8,128)(2,1)S(1)}, bf16[512,256]{1,0:T...) while((s32[]{:T(128)}, bf16[512,2048]{1,0:T(8,128)(2,1)S(1)}, ...), condition=%wide.region_7.8_spmd.clone, body=%wide.region_2.7_spmd.clone.sunk | while | flops 272563200 | bytes 7762787 | solution.py:67
  63.8 1.2 fusion.69
  66.1 1.2 fusion.68
  67.3 1.2 fusion.69
  69.7 1.2 fusion.68
  70.9 1.2 fusion.69
  73.3 1.2 fusion.68
  74.5 1.2 fusion.69
  76.8 1.2 fusion.68
  78.1 1.2 fusion.69
  80.4 1.2 fusion.68
  81.6 1.2 fusion.69
  84.0 1.2 fusion.68
  85.2 1.2 fusion.69
  88.8 1.2 fusion.69
  92.4 1.2 fusion.69
  95.9 1.2 fusion.69
  98.3 1.2 fusion.68
  99.5 1.2 fusion.69
  103.1 1.2 fusion.69
  106.7 1.2 fusion.69
  110.2 1.2 fusion.69
  112.6 1.2 fusion.68
  113.8 1.2 fusion.69
  117.4 1.2 fusion.69
  119.7 1.3 %copy-done.1 = bf16[512,2048]{1,0:T(8,128)(2,1)} copy-done((bf16[512,2048]{1,0:T(8,128)(2,1)}, bf16[512,2048]{1,0:T(8,128)(2,1)S(1)}, u32[]{:S(2)}) %copy-start.1) | copy-done | bytes 2097176
  (199 shorter events, 42.0 us)
Async XLA Ops:
  7.2 18.5 %copy-start.4 = (bf16[512,256]{1,0:T(8,128)(2,1)S(1)}, bf16[512,256]{1,0:T(8,128)(2,1)}, u32[]{:S(2)}) copy-start(bf16[512,256]{1,0:T(8,128)(2,1)} %param.13) | copy-start | bytes 786436
  7.2 18.5 %copy-start = (bf16[512,256]{1,0:T(8,128)(2,1)S(1)}, bf16[512,256]{1,0:T(8,128)(2,1)}, u32[]{:S(2)}) copy-start(bf16[512,256]{1,0:T(8,128)(2,1)} %param.12) | copy-start | bytes 786436
  7.2 54.3 %all-reduce.3.cloned.1.call-start = ((), (), s32[]{:S(2)}) async-start(), calls=%async_computation.2 | async-start | bytes 1048576 | tf_op jit(solution)/shard_map/psum | solution.py:14
  9.2 110.5 %reduce-scatter.2.cloned.1.call-start = ((), (), s32[]{:S(2)}) async-start(), calls=%async_computation.1 | async-start | bytes 655360 | tf_op jit(solution)/shard_map/reduce_scatter | solution.py:102
  25.7 33.3 %copy-start.6 = (s32[64]{0:T(128)S(1)}, s32[64]{0:T(128)}, u32[]{:S(2)}) copy-start(s32[64]{0:T(128)} %param.16) | copy-start | bytes 772
  25.7 33.3 %copy-start.7 = (s32[64]{0:T(128)S(1)}, s32[64]{0:T(128)}, u32[]{:S(2)}) copy-start(s32[64]{0:T(128)} %param.15) | copy-start | bytes 772
  61.4 0.9 copy-start.5
  61.5 1.0 copy-start.2
  61.5 1.1 copy-start.3
  119.7 1.3 %copy-start.1 = (bf16[512,2048]{1,0:T(8,128)(2,1)}, bf16[512,2048]{1,0:T(8,128)(2,1)S(1)}, u32[]{:S(2)}) copy-start(bf16[512,2048]{1,0:T(8,128)(2,1)S(1)} %get-tuple-element.421) | copy-start | bytes 6291460
Sparse Core Ops, SparseCore 0:
  11.0 43.1 all-reduce.2
  61.6 21.6 reduce-scatter.1
where the time goes:
time: 129 us; the launch traced here: 128 us
  matrix products  59.5 us (46%)
  blocking collectives  36 us (28%)
  between operations  14.2 us (11%)
  other arithmetic  13 us (10%)
  local copies, waits for them, and re-layouts  3.26 us (3%)
  loops' own time  1.7 us (1%)
    dot_general x48, matrix products, soft_parts(): jnp.einsum('td,sd->ts', query_head, key_part, preferred_element_type=jnp....  43.5 us
    dot_general x48, matrix products, soft_parts(): jnp.dot(expo.astype(jnp.bfloat16), value_part, preferred_element_type=jnp...  15.9 us
    all_gather x1, blocking collectives, body(): all_queries = lax.all_gather(opt_query, 'blk', axis=0, tiled=True)  15.8 us
    pmax x1, blocking collectives, body(): top_all = lax.pmax(stats, 'blk')  11.7 us
    psum x1, blocking collectives, body(): weight_sum = lax.psum(weight, 'blk')  8.52 us
    reduce_sum x32, other arithmetic, soft_parts(): total = total + jnp.sum(expo, axis=1)  7.92 us
  transfers between devices with their start and end apart: 2, of which 0 were waited for; matrix products, arithmetic and copies ran while one was open for 56% of the time, Pallas kernels for 0%

commit v1 on v0

v1 whole, which is shorter than its diff:
```python
import functools
import math

import jax
import jax.numpy as jnp
from jax import lax
from jax.experimental import pallas as pl
from jax.experimental.pallas import tpu as pltpu
from jax.sharding import PartitionSpec as P

HD = 128
HQ = 64
KVH = 8
CAP = 32
GROUP = HQ // KVH
MESH = pl.DeviceIdType.MESH
NEG = -1e30
LN2 = math.log(2.0)
COEF = HD**-0.5 / LN2
QUARTERS = 4
PAIR = 2


def dot_nt(a, b):
    return lax.dot_general(a, b, (((1,), (1,)), ((), ())), preferred_element_type=jnp.float32)


def dot_nn(a, b, precision=None):
    return lax.dot_general(
        a, b, (((1,), (0,)), ((), ())), preferred_element_type=jnp.float32, precision=precision
    )


def kernel(
    n,
    q_hbm, k_hbm, v_hbm, oq_hbm, len_ref, dest_ref,
    ctx_hbm, opt_ref,
    q_ref, k_ref, vx_ref, ak_ref, avx_ref, oq_ref, acc_ref, m_ref, out_ref,
    part_ref, stat_ref, pbuf, sbuf, rx_p, rx_s,
    q_sem, k_sem, v_sem, o_sem, out_sem,
    oq_send, oq_recv, ak_send, ak_recv, av_send, av_recv,
    p_send, p_recv, s_send, s_recv,
):
    me = lax.axis_index("blk")
    rows = q_ref.shape[0]
    heads = q_ref.shape[1] // HD
    kvs = k_ref.shape[1] // HD
    entry = oq_hbm.shape[0]
    opts = oq_ref.shape[0]
    chunk = rows // QUARTERS
    pairs = heads // PAIR
    per_group = GROUP // PAIR
    tile = rows // 2
    half = heads // 2 * HD

    q_copies = [
        pltpu.make_async_copy(
            q_hbm.at[:, pl.ds(s * half, half)], q_ref.at[:, pl.ds(s * half, half)], q_sem.at[s]
        )
        for s in range(2)
    ]
    k_copy = pltpu.make_async_copy(k_hbm, k_ref, k_sem)
    ones = jnp.ones((rows, HD), jnp.bfloat16)
    for g in range(kvs):
        vx_ref[g, :, HD:] = ones
        avx_ref[g, :, HD:] = ones
    v_copies = [
        pltpu.make_async_copy(
            v_hbm.at[:, pl.ds(g * HD, HD)], vx_ref.at[g, :, pl.ds(0, HD)], v_sem.at[g]
        )
        for g in range(kvs)
    ]
    own = pl.ds(pl.multiple_of(me * entry, entry), entry)
    o_copy = pltpu.make_async_copy(oq_hbm, oq_ref.at[own], o_sem)
    k_copy.start()
    for copy in v_copies:
        copy.start()
    q_copies[0].start()
    q_copies[1].start()
    o_copy.start()

    barrier = pltpu.get_barrier_semaphore()
    for step in range(1, n):
        pl.semaphore_signal(
            barrier, inc=1, device_id={"blk": lax.rem(me + step, n)}, device_id_type=MESH
        )
    pl.semaphore_wait(barrier, n - 1)

    def oq_copy(step):
        return pltpu.make_async_remote_copy(
            src_ref=oq_hbm,
            dst_ref=oq_ref.at[own],
            send_sem=oq_send.at[step - 1],
            recv_sem=oq_recv.at[step - 1],
            device_id={"blk": lax.rem(me + step, n)},
            device_id_type=MESH,
        )

    for step in range(1, n):
        oq_copy(step).start()

    k_copy.wait()
    for copy in v_copies:
        copy.wait()

    up = lax.rem(me + 1, n)

    def anchor_copies(c, from_own):
        g = c // QUARTERS
        r = lax.rem(c, QUARTERS)
        span = pl.ds(pl.multiple_of(r * chunk, chunk), chunk)
        cols = pl.ds(pl.multiple_of(g * HD, HD), HD)
        key_from = k_ref if from_own else ak_ref
        value_from = vx_ref if from_own else avx_ref
        return (
            pltpu.make_async_remote_copy(
                src_ref=key_from.at[span, cols],
                dst_ref=ak_ref.at[span, cols],
                send_sem=ak_send.at[c],
                recv_sem=ak_recv.at[c],
                device_id={"blk": up},
                device_id_type=MESH,
            ),
            pltpu.make_async_remote_copy(
                src_ref=value_from.at[g, span, pl.ds(0, HD)],
                dst_ref=avx_ref.at[g, span, pl.ds(0, HD)],
                send_sem=av_send.at[c],
                recv_sem=av_recv.at[c],
                device_id={"blk": up},
                device_id_type=MESH,
            ),
        )

    chunks = QUARTERS * kvs

    @pl.when(me == 0)
    def _():
        def send(c, carry):
            for copy in anchor_copies(c, True):
                copy.start()
            return carry

        lax.fori_loop(0, chunks, send, 0)

    def forward(c):
        @pl.when(me > 0)
        def _():
            for copy in anchor_copies(c, False):
                copy.wait_recv()

            @pl.when(me < n - 1)
            def _():
                for copy in anchor_copies(c, False):
                    copy.start()

    def head_cols(h):
        return pl.ds(pl.multiple_of(h * HD, HD), HD)

    diag_row = lax.broadcasted_iota(jnp.int32, (tile, tile), 0)
    diag_col = lax.broadcasted_iota(jnp.int32, (tile, tile), 1)
    causal = diag_row >= diag_col

    def local_head(h):
        g = h // GROUP
        for t in range(2):
            span = pl.ds(t * tile, tile)
            query = q_ref[span, head_cols(h)]
            diag = dot_nt(query, k_ref[span, head_cols(g)])
            diag = jnp.where(causal, diag, NEG)
            top = jnp.max(diag, axis=1, keepdims=True)
            if t:
                rest = dot_nt(query, k_ref[pl.ds(0, t * tile), head_cols(g)])
                top = jnp.maximum(top, jnp.max(rest, axis=1, keepdims=True))
            top = top * COEF
            acc = dot_nn(jnp.exp2(diag * COEF - top).astype(jnp.bfloat16), vx_ref[g, span, :])
            if t:
                acc = acc + dot_nn(
                    jnp.exp2(rest * COEF - top).astype(jnp.bfloat16),
                    vx_ref[g, pl.ds(0, t * tile), :],
                )
            acc_ref[h, span, :] = acc
            m_ref[h, span, :] = jnp.broadcast_to(top, (tile, HD))

    def anchor_head(h):
        g = h // GROUP
        for t in range(2):
            span = pl.ds(t * tile, tile)
            query = q_ref[span, head_cols(h)]
            score = dot_nt(query, ak_ref[:, head_cols(g)])
            before = m_ref[h, span, :]
            top = jnp.maximum(jnp.max(score, axis=1, keepdims=True) * COEF, before[:, :1])
            acc = dot_nn(jnp.exp2(score * COEF - top).astype(jnp.bfloat16), avx_ref[g])
            alpha = jnp.exp2(before - top)
            value = acc[:, :HD] + alpha * acc_ref[h, span, pl.ds(0, HD)]
            total = acc[:, HD:] + alpha * acc_ref[h, span, pl.ds(HD, HD)]
            out_ref[span, head_cols(h)] = (value / total).astype(jnp.bfloat16)

    offset = pairs - QUARTERS

    def local_pair(i, carry):
        for j in range(PAIR):
            local_head(i * PAIR + j)

        @pl.when(i >= offset)
        def _():
            forward(i - offset)

        return carry

    dest = dest_ref[...]
    length = len_ref[...].astype(jnp.float32)

    def opt_attend(queries, count, key, value_x):
        size = queries.shape[0]
        stacked = jnp.concatenate([queries[:, j * HD : (j + 1) * HD] for j in range(GROUP)], axis=0)
        counts = jnp.concatenate([count] * GROUP, axis=0)
        score = dot_nt(stacked, key)
        spot = lax.broadcasted_iota(jnp.int32, score.shape, 1).astype(jnp.float32)
        score = jnp.where(spot < counts, score, NEG)
        top = jnp.max(score, axis=1, keepdims=True) * COEF
        acc = dot_nn(jnp.exp2(score * COEF - top).astype(jnp.bfloat16), value_x)
        total = acc[:, HD:]
        live = counts > 0.0
        part = jnp.where(live, acc[:, :HD] / total, 0.0).astype(jnp.bfloat16)
        stat = jnp.where(live, top * LN2 + jnp.log(total), NEG)
        return (
            [part[j * size : (j + 1) * size] for j in range(GROUP)],
            [stat[j * size : (j + 1) * size] for j in range(GROUP)],
        )

    step_rows = min(opts, 64)

    def options_blk():
        for base in range(0, opts, step_rows):
            span = pl.ds(base, step_rows)
            eye = lax.broadcasted_iota(jnp.int32, (step_rows, opts), 0) + base
            eye = eye == lax.broadcasted_iota(jnp.int32, (step_rows, opts), 1)
            col = jnp.sum(jnp.where(eye, length, 0.0), axis=1, keepdims=True)
            start = (me * rows).astype(jnp.float32)
            count = jnp.clip(col - start, 0.0, float(rows))
            lanes = lax.broadcasted_iota(jnp.int32, (step_rows, HD), 1)
            stats = jnp.zeros((step_rows, HD), jnp.float32)
            for g in range(kvs):
                queries = oq_ref[span, pl.ds(g * GROUP * HD, GROUP * HD)]
                parts, tops = opt_attend(queries, count, k_ref[:, pl.ds(g * HD, HD)], vx_ref[g])
                for j in range(GROUP):
                    h = g * GROUP + j
                    part_ref[span, pl.ds(h * HD, HD)] = parts[j]
                    stats = jnp.where(lanes == h, tops[j], stats)
            stat_ref[span, :] = stats
        slots = lax.broadcasted_iota(jnp.int32, (CAP, opts), 0)
        for d in range(n):
            hot = (slots + d * CAP == dest).astype(jnp.float32)
            span = pl.ds(d * CAP, CAP)
            pbuf[span, :] = dot_nn(hot.astype(jnp.bfloat16), part_ref[...]).astype(jnp.bfloat16)
            sbuf[span, :] = dot_nn(hot, stat_ref[...], lax.Precision.HIGHEST)

    def part_copies(step):
        to = lax.rem(me + step, n)
        span = pl.ds(pl.multiple_of(to * CAP, CAP), CAP)
        return (
            pltpu.make_async_remote_copy(
                src_ref=pbuf.at[span],
                dst_ref=rx_p.at[me],
                send_sem=p_send.at[step - 1],
                recv_sem=p_recv.at[step - 1],
                device_id={"blk": to},
                device_id_type=MESH,
            ),
            pltpu.make_async_remote_copy(
                src_ref=sbuf.at[span],
                dst_ref=rx_s.at[me],
                send_sem=s_send.at[step - 1],
                recv_sem=s_recv.at[step - 1],
                device_id={"blk": to},
                device_id_type=MESH,
            ),
        )

    mine_hot = (lax.broadcasted_iota(jnp.int32, (CAP, opts), 0) + me * CAP) == dest

    def options_anchor(key_of, value_of):
        count = jnp.sum(jnp.where(mine_hot, length, 0.0), axis=1, keepdims=True)
        count = jnp.clip(count, 0.0, float(rows))
        hot = mine_hot.astype(jnp.float32).astype(jnp.bfloat16)
        lanes = lax.broadcasted_iota(jnp.int32, (CAP, HD), 1)
        stats = jnp.zeros((CAP, HD), jnp.float32)
        for g in range(kvs):
            cols = pl.ds(g * GROUP * HD, GROUP * HD)
            queries = dot_nn(hot, oq_ref[:, cols]).astype(jnp.bfloat16)
            parts, tops = opt_attend(queries, count, key_of[:, pl.ds(g * HD, HD)], value_of[g])
            for j in range(GROUP):
                h = g * GROUP + j
                rx_p[0, :, pl.ds(h * HD, HD)] = parts[j]
                stats = jnp.where(lanes == h, tops[j], stats)
        rx_s[0] = stats

    cut = pairs // 2
    for copy in q_copies:
        copy.wait()
    lax.fori_loop(0, cut, local_pair, 0)
    o_copy.wait()
    for step in range(1, n):
        oq_copy(step).wait()

    @pl.when(me > 0)
    def _():
        options_blk()

    lax.fori_loop(cut, pairs, local_pair, 0)

    @pl.when(me > 0)
    def _():
        for step in range(1, n):
            for copy in part_copies(step):
                copy.start()
        own_slots = pl.ds(pl.multiple_of(me * CAP, CAP), CAP)
        rx_p[me] = pbuf[own_slots, :]
        rx_s[me] = sbuf[own_slots, :]

    def out_copy(i):
        cols = pl.ds(pl.multiple_of(i * PAIR * HD, PAIR * HD), PAIR * HD)
        return pltpu.make_async_copy(out_ref.at[:, cols], ctx_hbm.at[:, cols], out_sem.at[i])

    @pl.when(me == 0)
    def _():
        def finish(i, carry):
            for j in range(PAIR):
                h = i * PAIR + j
                out_ref[:, head_cols(h)] = (
                    acc_ref[h, :, pl.ds(0, HD)] / acc_ref[h, :, pl.ds(HD, HD)]
                ).astype(jnp.bfloat16)
            out_copy(i).start()
            return carry

        lax.fori_loop(0, pairs, finish, 0)
        options_anchor(k_ref, vx_ref)

    @pl.when(me > 0)
    def _():
        def finish(i, carry):
            for j in range(PAIR):
                anchor_head(i * PAIR + j)
            out_copy(i).start()

            @pl.when(i + QUARTERS < chunks)
            def _():
                forward(i + QUARTERS)

            return carry

        lax.fori_loop(0, pairs, finish, 0)
        options_anchor(ak_ref, avx_ref)

    for step in range(1, n):
        @pl.when(lax.rem(me - step + n, n) > 0)
        def _():
            for copy in part_copies(step):
                copy.wait_recv()

    top = rx_s[0]
    for b in range(1, n):
        top = jnp.maximum(top, rx_s[b])
    total = jnp.zeros_like(top)
    for b in range(n):
        total = total + jnp.exp(rx_s[b] - top)
    occupied = jnp.sum(mine_hot.astype(jnp.float32), axis=1, keepdims=True) > 0.0
    for h in range(heads):
        cols = pl.ds(h * HD, HD)
        merged = jnp.zeros((CAP, HD), jnp.float32)
        for b in range(n):
            weight = jnp.exp(rx_s[b, :, pl.ds(h, 1)] - top[:, h : h + 1])
            merged = merged + weight * rx_p[b, :, cols].astype(jnp.float32)
        merged = merged / total[:, h : h + 1]
        opt_ref[:, cols] = jnp.where(occupied, merged, 0.0).astype(jnp.bfloat16)

    @pl.when(me == 0)
    def _():
        def drain(c, carry):
            for copy in anchor_copies(c, True):
                copy.wait_send()
            return carry

        lax.fori_loop(0, chunks, drain, 0)

    @pl.when((me > 0) & (me < n - 1))
    def _():
        def drain(c, carry):
            for copy in anchor_copies(c, False):
                copy.wait_send()
            return carry

        lax.fori_loop(0, chunks, drain, 0)

    @pl.when(me > 0)
    def _():
        for step in range(1, n):
            for copy in part_copies(step):
                copy.wait_send()

    def drain_out(i, carry):
        out_copy(i).wait()
        return carry

    lax.fori_loop(0, pairs, drain_out, 0)


def body(ctx_query, ctx_key, ctx_value, opt_query, opt_owner, opt_slot, opt_length):
    n = lax.axis_size("blk")
    rows, width = ctx_query.shape
    heads = width // HD
    kvs = ctx_key.shape[1] // HD
    opts = opt_length.shape[0]
    entry = opt_query.shape[0]
    chunks = QUARTERS * kvs
    dest = (opt_owner * CAP + opt_slot).reshape(1, opts)
    bf16, f32 = jnp.bfloat16, jnp.float32
    dma = pltpu.SemaphoreType.DMA
    hbm = pl.BlockSpec(memory_space=pl.ANY)
    vmem = pl.BlockSpec(memory_space=pltpu.VMEM)
    return pl.pallas_call(
        functools.partial(kernel, n),
        out_shape=(
            jax.ShapeDtypeStruct((rows, width), bf16),
            jax.ShapeDtypeStruct((CAP, width), bf16),
        ),
        in_specs=[hbm, hbm, hbm, hbm, vmem, vmem],
        out_specs=(hbm, vmem),
        scratch_shapes=[
            pltpu.VMEM((rows, width), bf16),
            pltpu.VMEM((rows, kvs * HD), bf16),
            pltpu.VMEM((kvs, rows, 2 * HD), bf16),
            pltpu.VMEM((rows, kvs * HD), bf16),
            pltpu.VMEM((kvs, rows, 2 * HD), bf16),
            pltpu.VMEM((opts, width), bf16),
            pltpu.VMEM((heads, rows, 2 * HD), f32),
            pltpu.VMEM((heads, rows, HD), f32),
            pltpu.VMEM((rows, width), bf16),
            pltpu.VMEM((opts, width), bf16),
            pltpu.VMEM((opts, HD), f32),
            pltpu.VMEM((n * CAP, width), bf16),
            pltpu.VMEM((n * CAP, HD), f32),
            pltpu.VMEM((n, CAP, width), bf16),
            pltpu.VMEM((n, CAP, HD), f32),
            dma((2,)), dma(()), dma((kvs,)), dma(()), dma((heads // PAIR,)),
            dma((n - 1,)), dma((n - 1,)),
            dma((chunks,)), dma((chunks,)), dma((chunks,)), dma((chunks,)),
            dma((n - 1,)), dma((n - 1,)), dma((n - 1,)), dma((n - 1,)),
        ],
        compiler_params=pltpu.CompilerParams(
            collective_id=0, has_side_effects=True, vmem_limit_bytes=60 * 1024 * 1024
        ),
        name="star",
    )(ctx_query, ctx_key, ctx_value, opt_query, opt_length.reshape(1, opts), dest)


def solution(mesh):
    return jax.shard_map(
        body,
        mesh=mesh,
        in_specs=(
            P(("groups", "blk"), "head"),
            P(("groups", "blk"), "head"),
            P(("groups", "blk"), "head"),
            P(("groups", "blk"), "head"),
            P("groups"),
            P("groups"),
            P("groups"),
        ),
        out_specs=(P(("groups", "blk"), "head"), P(("groups", "blk"), "head")),
        check_vma=False,
    )
```

time: 129 us -> 49.5 us (0.38)
  the two profiles are of different devices: /device:TPU:0 before, /device:TPU:26 now
where the time goes in v1:
time: 49.5 us; the launch traced here: 49.3 us
  Pallas kernels  43.6 us (88%)
  local copies, waits for them, and re-layouts  3.85 us (8%)
  other arithmetic  1.19 us (2%)
  between operations  0.65 us (1%)
    pallas_call x1, Pallas kernels, body(): pl.pallas_call(functools.partial(kernel, n), out_shape=(jax.ShapeDtypeStr...  43.6 us
    unnamed x4, local copies, waits for them, and re-layouts  3.85 us
    reshape x1, other arithmetic, body(): dest = (opt_owner * CAP + opt_slot).reshape(1, opts)  1.19 us

profile of v1, /device:TPU:26, one launch (start us, length us, event | category | flops | bytes accessed | tf_op | source)
XLA Modules:
  0.0 49.3 jit_solution(14843786280021023383)
XLA Ops:
  0.6 1.2 %add_bitcast_fusion.dest_ref = s32[1,64]{1,0:T(1,128)} fusion(s32[64]{0:T(128)} %param.12, s32[64]{0:T(128)} %param.11), kind=kLoop, calls=%fused_computation | loop fusion | flops 128 | bytes 768 | tf_op jit(solution)/shard_map/reshape | solution.py:416
  1.8 43.6 %star.1 = (bf16[512,2048]{1,0:T(8,128)(2,1)}, bf16[32,2048]{1,0:T(8,128)(2,1)}) custom-call(bf16[512,2048]{1,0:T(8,128)(2,1)} %q_hbm.1, bf16[512,256]{1,0:T(8,128)(2,1)} %k_hbm.1, bf16[512,256]{1,0:T(8,128)(2,1)} %v_hbm.1, bf16[16,2048]{1,0:T(8,128)(2,1)} %oq_hbm.1, s32[1,64]{1,0:T(1,128)} %bitcast.3, s32[1,64]{1,0:T(1,128)} %add_bitcast_fusion.dest_ref), custom_call_target="tpu_custom_call" | custom-call | tf_op jit(solution)/shard_map/star/pallas_call | solution.py:421
  45.4 0.0 copy-start
  45.4 3.2 %copy.11 = bf16[512,2048]{1,0:T(8,128)(2,1)} copy(bf16[512,2048]{1,0:T(8,128)(2,1)} %get-tuple-element.4) | data formatting | bytes 4194304
  48.6 0.0 copy-done
  48.6 0.7 %copy.12 = bf16[32,2048]{1,0:T(8,128)(2,1)} copy(bf16[32,2048]{1,0:T(8,128)(2,1)S(1)} %copy-done) | data formatting | bytes 262144
Async XLA Ops:
  45.4 3.2 %copy-start = (bf16[32,2048]{1,0:T(8,128)(2,1)S(1)}, bf16[32,2048]{1,0:T(8,128)(2,1)}, u32[]{:S(2)}) copy-start(bf16[32,2048]{1,0:T(8,128)(2,1)} %get-tuple-element.5) | copy-start | bytes 393220

commit v2 on v1

--- a/solution.py
+++ b/solution.py
@@ -33,12 +33,12 @@
 
 def kernel(
     n,
-    q_hbm, k_hbm, v_hbm, oq_hbm, len_ref, dest_ref,
+    q_hbm, k_hbm, v_hbm, oq_hbm, len_ref, owner_ref, slot_ref,
     ctx_hbm, opt_ref,
     q_ref, k_ref, vx_ref, ak_ref, avx_ref, oq_ref, acc_ref, m_ref, out_ref,
     part_ref, stat_ref, pbuf, sbuf, rx_p, rx_s,
     q_sem, k_sem, v_sem, o_sem, out_sem,
-    oq_send, oq_recv, ak_send, ak_recv, av_send, av_recv,
+    oq_send, oq_recv, ou_send, ou_recv, ak_send, ak_recv, av_send, av_recv,
     p_send, p_recv, s_send, s_recv,
 ):
     me = lax.axis_index("blk")
@@ -86,18 +86,43 @@
         )
     pl.semaphore_wait(barrier, n - 1)
 
-    def oq_copy(step):
+    def oq_down(step):
         return pltpu.make_async_remote_copy(
             src_ref=oq_hbm,
             dst_ref=oq_ref.at[own],
             send_sem=oq_send.at[step - 1],
             recv_sem=oq_recv.at[step - 1],
-            device_id={"blk": lax.rem(me + step, n)},
+            device_id={"blk": lax.rem(me - step + n, n)},
             device_id_type=MESH,
         )
 
+    def oq_up(step):
+        at = lax.rem(me - step + 1 + n, n)
+        span = pl.ds(pl.multiple_of(at * entry, entry), entry)
+        return pltpu.make_async_remote_copy(
+            src_ref=oq_hbm if step == 1 else oq_ref.at[span],
+            dst_ref=oq_ref.at[span],
+            send_sem=ou_send.at[step - 1],
+            recv_sem=ou_recv.at[step - 1],
+            device_id={"blk": lax.rem(me + 1, n)},
+            device_id_type=MESH,
+        )
+
+    def oq_up_arrived(step):
+        @pl.when(me >= step)
+        def _():
+            oq_up(step).wait_recv()
+
+    def oq_up_start(step):
+        @pl.when((me >= step - 1) & (me < n - 1))
+        def _():
+            oq_up(step).start()
+
+    oq_up_start(1)
     for step in range(1, n):
-        oq_copy(step).start()
+        @pl.when(me >= step)
+        def _():
+            oq_down(step).start()
 
     k_copy.wait()
     for copy in v_copies:
@@ -160,54 +185,87 @@
     diag_col = lax.broadcasted_iota(jnp.int32, (tile, tile), 1)
     causal = diag_row >= diag_col
 
-    def local_head(h):
-        g = h // GROUP
-        for t in range(2):
+    def local_heads(hs):
+        units = [(h, t) for h in hs for t in range(2)]
+        raw, tops, probs = {}, {}, {}
+
+        def scores(u):
+            h, t = units[u]
+            g = h // GROUP
+            query = q_ref[pl.ds(t * tile, tile), head_cols(h)]
+            parts = [dot_nt(query, k_ref[pl.ds(j * tile, tile), head_cols(g)]) for j in range(t + 1)]
+            parts[t] = jnp.where(causal, parts[t], NEG)
+            top = functools.reduce(jnp.maximum, parts)
+            tops[u] = jnp.max(top, axis=1, keepdims=True) * COEF
+            raw[u] = parts
+
+        def soften(u):
+            probs[u] = [jnp.exp2(x * COEF - tops[u]).astype(jnp.bfloat16) for x in raw.pop(u)]
+
+        def gather(u):
+            h, t = units[u]
+            g = h // GROUP
             span = pl.ds(t * tile, tile)
-            query = q_ref[span, head_cols(h)]
-            diag = dot_nt(query, k_ref[span, head_cols(g)])
-            diag = jnp.where(causal, diag, NEG)
-            top = jnp.max(diag, axis=1, keepdims=True)
-            if t:
-                rest = dot_nt(query, k_ref[pl.ds(0, t * tile), head_cols(g)])
-                top = jnp.maximum(top, jnp.max(rest, axis=1, keepdims=True))
-            top = top * COEF
-            acc = dot_nn(jnp.exp2(diag * COEF - top).astype(jnp.bfloat16), vx_ref[g, span, :])
-            if t:
-                acc = acc + dot_nn(
-                    jnp.exp2(rest * COEF - top).astype(jnp.bfloat16),
-                    vx_ref[g, pl.ds(0, t * tile), :],
-                )
-            acc_ref[h, span, :] = acc
-            m_ref[h, span, :] = jnp.broadcast_to(top, (tile, HD))
-
-    def anchor_head(h):
-        g = h // GROUP
-        for t in range(2):
+            prob = jnp.concatenate(probs.pop(u), axis=1)
+            acc_ref[h, span, :] = dot_nn(prob, vx_ref[g, pl.ds(0, (t + 1) * tile), :])
+            m_ref[h, span, :] = jnp.broadcast_to(tops[u], (tile, HD))
+
+        staged(units, scores, soften, gather)
+
+    def staged(units, scores, soften, gather):
+        count = len(units)
+        for k in range(count + 2):
+            if k < count:
+                scores(k)
+            if 0 <= k - 1 < count:
+                soften(k - 1)
+            if 0 <= k - 2 < count:
+                gather(k - 2)
+
+    def anchor_heads(hs):
+        units = [(h, t) for h in hs for t in range(2)]
+        raw, tops, probs = {}, {}, {}
+
+        def scores(u):
+            h, t = units[u]
             span = pl.ds(t * tile, tile)
-            query = q_ref[span, head_cols(h)]
-            score = dot_nt(query, ak_ref[:, head_cols(g)])
-            before = m_ref[h, span, :]
-            top = jnp.maximum(jnp.max(score, axis=1, keepdims=True) * COEF, before[:, :1])
-            acc = dot_nn(jnp.exp2(score * COEF - top).astype(jnp.bfloat16), avx_ref[g])
-            alpha = jnp.exp2(before - top)
+            raw[u] = dot_nt(q_ref[span, head_cols(h)], ak_ref[:, head_cols(h // GROUP)])
+            top = jnp.max(raw[u], axis=1, keepdims=True) * COEF
+            tops[u] = jnp.maximum(top, m_ref[h, span, :][:, :1])
+
+        def soften(u):
+            probs[u] = jnp.exp2(raw.pop(u) * COEF - tops[u]).astype(jnp.bfloat16)
+
+        def gather(u):
+            h, t = units[u]
+            span = pl.ds(t * tile, tile)
+            acc = dot_nn(probs.pop(u), avx_ref[h // GROUP])
+            alpha = jnp.exp2(m_ref[h, span, :] - tops[u])
             value = acc[:, :HD] + alpha * acc_ref[h, span, pl.ds(0, HD)]
             total = acc[:, HD:] + alpha * acc_ref[h, span, pl.ds(HD, HD)]
             out_ref[span, head_cols(h)] = (value / total).astype(jnp.bfloat16)
 
-    offset = pairs - QUARTERS
+        staged(units, scores, soften, gather)
+
+    cut = pairs - 1
+    offset = max(pairs - QUARTERS - 1, 0) + 2 * (me - 1)
 
     def local_pair(i, carry):
-        for j in range(PAIR):
-            local_head(i * PAIR + j)
-
-        @pl.when(i >= offset)
+        local_heads([i * PAIR + j for j in range(PAIR)])
+
+        for step in range(1, n - 1):
+            @pl.when(i == min(2 * step, cut - 1))
+            def _():
+                oq_up_arrived(step)
+                oq_up_start(step + 1)
+
+        @pl.when((me > 0) & (i >= offset) & (i < offset + chunks))
         def _():
             forward(i - offset)
 
         return carry
 
-    dest = dest_ref[...]
+    dest = owner_ref[...] * CAP + slot_ref[...]
     length = len_ref[...].astype(jnp.float32)
 
     def opt_attend(queries, count, key, value_x):
@@ -295,13 +353,15 @@
                 stats = jnp.where(lanes == h, tops[j], stats)
         rx_s[0] = stats
 
-    cut = pairs // 2
     for copy in q_copies:
         copy.wait()
     lax.fori_loop(0, cut, local_pair, 0)
     o_copy.wait()
+    oq_up_arrived(n - 1)
     for step in range(1, n):
-        oq_copy(step).wait()
+        @pl.when(me + step < n)
+        def _():
+            oq_down(step).wait_recv()
 
     @pl.when(me > 0)
     def _():
@@ -309,11 +369,21 @@
 
     lax.fori_loop(cut, pairs, local_pair, 0)
 
+    def send_parts(upward):
+        for step in range(1, n):
+            @pl.when((me + step < n) if upward else (me + step >= n))
+            def _():
+                for copy in part_copies(step):
+                    copy.start()
+
     @pl.when(me > 0)
     def _():
-        for step in range(1, n):
-            for copy in part_copies(step):
-                copy.start()
+        send_parts(False)
+        for c in range(QUARTERS):
+            @pl.when(c + offset >= pairs)
+            def _():
+                forward(c)
+
         own_slots = pl.ds(pl.multiple_of(me * CAP, CAP), CAP)
         rx_p[me] = pbuf[own_slots, :]
         rx_s[me] = sbuf[own_slots, :]
@@ -339,13 +409,18 @@
     @pl.when(me > 0)
     def _():
         def finish(i, carry):
-            for j in range(PAIR):
-                anchor_head(i * PAIR + j)
+            anchor_heads([i * PAIR + j for j in range(PAIR)])
             out_copy(i).start()
 
-            @pl.when(i + QUARTERS < chunks)
+            at = i + jnp.maximum(pairs - offset, QUARTERS)
+
+            @pl.when(at < chunks)
             def _():
-                forward(i + QUARTERS)
+                forward(at)
+
+            @pl.when(i == max(chunks - QUARTERS - 1, 0))
+            def _():
+                send_parts(True)
 
             return carry
 
@@ -374,6 +449,15 @@
         merged = merged / total[:, h : h + 1]
         opt_ref[:, cols] = jnp.where(occupied, merged, 0.0).astype(jnp.bfloat16)
 
+    for step in range(1, n):
+        @pl.when(me >= step)
+        def _():
+            oq_down(step).wait_send()
+
+        @pl.when((me >= step - 1) & (me < n - 1))
+        def _():
+            oq_up(step).wait_send()
+
     @pl.when(me == 0)
     def _():
         def drain(c, carry):
@@ -413,7 +497,6 @@
     opts = opt_length.shape[0]
     entry = opt_query.shape[0]
     chunks = QUARTERS * kvs
-    dest = (opt_owner * CAP + opt_slot).reshape(1, opts)
     bf16, f32 = jnp.bfloat16, jnp.float32
     dma = pltpu.SemaphoreType.DMA
     hbm = pl.BlockSpec(memory_space=pl.ANY)
@@ -424,7 +507,7 @@
             jax.ShapeDtypeStruct((rows, width), bf16),
             jax.ShapeDtypeStruct((CAP, width), bf16),
         ),
-        in_specs=[hbm, hbm, hbm, hbm, vmem, vmem],
+        in_specs=[hbm, hbm, hbm, hbm, vmem, vmem, vmem],
         out_specs=(hbm, vmem),
         scratch_shapes=[
             pltpu.VMEM((rows, width), bf16),
@@ -443,7 +526,7 @@
             pltpu.VMEM((n, CAP, width), bf16),
             pltpu.VMEM((n, CAP, HD), f32),
             dma((2,)), dma(()), dma((kvs,)), dma(()), dma((heads // PAIR,)),
-            dma((n - 1,)), dma((n - 1,)),
+            dma((n - 1,)), dma((n - 1,)), dma((n - 1,)), dma((n - 1,)),
             dma((chunks,)), dma((chunks,)), dma((chunks,)), dma((chunks,)),
             dma((n - 1,)), dma((n - 1,)), dma((n - 1,)), dma((n - 1,)),
         ],
@@ -451,7 +534,7 @@
             collective_id=0, has_side_effects=True, vmem_limit_bytes=60 * 1024 * 1024
         ),
         name="star",
-    )(ctx_query, ctx_key, ctx_value, opt_query, opt_length.reshape(1, opts), dest)
+    )(ctx_query, ctx_key, ctx_value, opt_query, *(x.reshape(1, opts) for x in (opt_length, opt_owner, opt_slot)))
 
 
 def solution(mesh):

time: 49.5 us -> 43.6 us (0.88)
  Pallas kernels: 43.6 us -> 38.9 us
  other arithmetic: 1.19 us -> 0 us
    pallas_call x1, Pallas kernels: 43.6 us -> 38.9 us  [body(): pl.pallas_call(functools.partial(kernel, n), out_shape=(jax.ShapeDtypeStr...]
    reshape x1 -> x0, other arithmetic: 1.19 us -> none  [body(): dest = (opt_owner * CAP + opt_slot).reshape(1, opts)]
where the time goes in v2:
time: 43.6 us; the launch traced here: 43.4 us
  Pallas kernels  38.9 us (89%)
  local copies, waits for them, and re-layouts  3.85 us (9%)
  between operations  0.65 us (1%)
    pallas_call x1, Pallas kernels, body(): pl.pallas_call(functools.partial(kernel, n), out_shape=(jax.ShapeDtypeStr...  38.9 us
    unnamed x4, local copies, waits for them, and re-layouts  3.85 us

profile of v2, /device:TPU:26, one launch (start us, length us, event | category | flops | bytes accessed | tf_op | source)
XLA Modules:
  0.0 43.4 jit_solution(4507850911263570565)
XLA Ops:
  0.6 38.9 %star.1 = (bf16[512,2048]{1,0:T(8,128)(2,1)}, bf16[32,2048]{1,0:T(8,128)(2,1)}) custom-call(bf16[512,2048]{1,0:T(8,128)(2,1)} %q_hbm.1, bf16[512,256]{1,0:T(8,128)(2,1)} %k_hbm.1, bf16[512,256]{1,0:T(8,128)(2,1)} %v_hbm.1, bf16[16,2048]{1,0:T(8,128)(2,1)} %oq_hbm.1, s32[1,64]{1,0:T(1,128)} %bitcast.3, s32[1,64]{1,0:T(1,128)} %bitcast.4, s32[1,64]{1,0:T(1,128)} %bitcast.5), custom_call_target="tpu_custom_call" | custom-call | tf_op jit(solution)/shard_map/star/pallas_call | solution.py:504
  39.5 0.0 copy-start
  39.5 3.2 %copy.11 = bf16[512,2048]{1,0:T(8,128)(2,1)} copy(bf16[512,2048]{1,0:T(8,128)(2,1)} %get-tuple-element.4) | data formatting | bytes 4194304
  42.7 0.0 copy-done
  42.7 0.7 %copy.12 = bf16[32,2048]{1,0:T(8,128)(2,1)} copy(bf16[32,2048]{1,0:T(8,128)(2,1)S(1)} %copy-done) | data formatting | bytes 262144
Async XLA Ops:
  39.5 3.2 %copy-start = (bf16[32,2048]{1,0:T(8,128)(2,1)S(1)}, bf16[32,2048]{1,0:T(8,128)(2,1)}, u32[]{:S(2)}) copy-start(bf16[32,2048]{1,0:T(8,128)(2,1)} %get-tuple-element.5) | copy-start | bytes 393220
